TPU v7x, 256 devices: a whole 4x4x8 slice. The times are simulated.
256 devices in a mesh: patch: 16 (over z_hi, x), wrow: 4 (over z_lo, core), wcol: 4 (over y).
Axes of the slice: x: 4, y: 4, z: 8 (z_hi: 4, z_lo: 2; z = z_hi * 2 + z_lo), core: 2. Of those that a mesh axis runs over, the one named last changes fastest.
Arguments:
- hidden_states: bfloat16 [4, 8192, 1536], P('wrow', ('patch', 'wcol')), may hold values from -6 to 6
- modulation: float32 [4, 3, 1536], P('wrow'), may hold values from -4 to 4
- w_qkv: bfloat16 [1536, 3, 1536], P('wrow', None, 'wcol'), may hold values from -1 to 1
- w_out: bfloat16 [1536, 1536], P('wcol', 'wrow'), may hold values from -0.15625 to 0.15625
- lengths: int32 [4], P('wrow'), may hold values from 1 to 8192, 20480 in all
Outputs:
- updated: bfloat16 [4, 8192, 1536], P('wrow', ('patch', 'wcol'))
Inputs may be any that keep to these rules, and one draw needn't show every extreme that they name: lengths[v] real tokens in video v, padding after them; the longest video fills all 8192 slots.
All inputs are finite; a program needn't handle non-finite values. No bound on the sum of `lengths` on one device may be relied on, other than what follows from the above.
Results may differ from a plain program's by a relative error of at most 0.015.
The roundings to bfloat16 on the way count: a program that leaves them out, or rounds other values in their place, can miss the bound.
Values may be sent and summed in bfloat16 or wider, within the bound.
A program may use at most 64 MiB of HBM per device.

v0:
```python
import jax
import jax.numpy as jnp
from jax import lax
from jax.sharding import PartitionSpec as P

HD = 128
EPSILON = 1e-06
FLOOR = -1e30


def modulated_norm(states, shift, scale):
    values = states.astype(jnp.float32)
    center = jnp.mean(values, axis=-1, keepdims=True)
    spread = jnp.mean(jnp.square(values - center), axis=-1, keepdims=True)
    return ((values - center) * lax.rsqrt(spread + EPSILON) * (1.0 + scale) + shift).astype(
        jnp.bfloat16
    )


def absorb(carry, keys, values, first, queries, limits):
    peak, weight_sum, numer = carry
    videos_here = keys.shape[0]
    count = keys.shape[1]
    heads_here = queries.shape[2]
    head_size = queries.shape[3]
    key_heads = keys.reshape(videos_here, count, heads_here, head_size)
    value_heads = values.reshape(videos_here, count, heads_here, head_size)
    scores = jnp.einsum(
        "vqhd,vkhd->vhqk", queries, key_heads, preferred_element_type=jnp.float32
    ) * head_size ** (-0.5)
    position = first + jnp.arange(count, dtype=jnp.int32)
    valid = (position[None, :] < limits[:, None])[:, None, None, :]
    scores = jnp.where(valid, scores, FLOOR)
    new_peak = jnp.maximum(peak, jnp.max(scores, axis=-1))
    factor = jnp.exp(peak - new_peak)
    probs = jnp.exp(scores - new_peak[..., None]) * valid.astype(jnp.float32)
    weight_sum = weight_sum * factor + jnp.sum(probs, axis=-1)
    numer = numer * factor[..., None] + jnp.einsum(
        "vhqk,vkhd->vhqd",
        probs.astype(jnp.bfloat16),
        value_heads,
        preferred_element_type=jnp.float32,
    )
    return (new_peak, weight_sum, numer)


def body(hidden_states, modulation, w_qkv, w_out, lengths):
    videos_here = hidden_states.shape[0]
    width = hidden_states.shape[2]
    shift = modulation[:, 0][:, None, :]
    scale = modulation[:, 1][:, None, :]
    gate = modulation[:, 2][:, None, :]
    normed = modulated_norm(hidden_states, shift, scale)
    tile_rows = lax.all_gather(normed, "wcol", axis=1, tiled=True)
    tile_len = tile_rows.shape[1]
    local_cols = w_qkv.shape[2]
    flat_rows = tile_rows.reshape(videos_here * tile_len, width)
    piece = lax.all_gather(w_qkv, "wrow", axis=0, tiled=True)
    mixed = jnp.dot(
        flat_rows, piece.reshape(piece.shape[0], 3 * local_cols), preferred_element_type=jnp.float32
    )
    mixed = mixed.reshape(videos_here, tile_len, 3 * local_cols)
    mixed = mixed.astype(jnp.bfloat16).reshape(videos_here, tile_len, 3, local_cols)
    heads_here = local_cols // HD
    queries = mixed[:, :, 0].reshape(videos_here, tile_len, heads_here, HD)
    keys = mixed[:, :, 1]
    values = mixed[:, :, 2]
    start_peak = jnp.full((videos_here, heads_here, tile_len), FLOOR, jnp.float32)
    start_sum = jnp.zeros((videos_here, heads_here, tile_len), jnp.float32)
    start_numer = jnp.zeros((videos_here, heads_here, tile_len, HD), jnp.float32)
    key_piece = lax.all_gather(keys, "patch", axis=1, tiled=True)
    value_piece = lax.all_gather(values, "patch", axis=1, tiled=True)
    count = key_piece.shape[1]
    block_len = 512

    def one_block(index, inner):
        offset = index * block_len
        key_block = lax.dynamic_slice_in_dim(key_piece, offset, block_len, 1)
        value_block = lax.dynamic_slice_in_dim(value_piece, offset, block_len, 1)
        return absorb(inner, key_block, value_block, offset, queries, lengths)

    peak, weight_sum, numer = lax.fori_loop(
        0, count // block_len, one_block, (start_peak, start_sum, start_numer)
    )
    attended = (numer / weight_sum[..., None]).astype(jnp.bfloat16)
    attended = jnp.transpose(attended, (0, 2, 1, 3)).reshape(videos_here * tile_len, local_cols)
    partial_out = jnp.dot(
        attended,
        lax.all_gather(w_out, "wrow", axis=1, tiled=True),
        preferred_element_type=jnp.float32,
    )
    partial_out = partial_out.reshape(videos_here, tile_len, width)
    out_proj = lax.psum_scatter(
        partial_out.astype(jnp.bfloat16), "wcol", scatter_dimension=1, tiled=True
    ).astype(jnp.float32)
    return (hidden_states.astype(jnp.float32) + gate * out_proj).astype(jnp.bfloat16)


def solution(mesh):
    placed = (
        P("wrow", ("patch", "wcol"), None),
        P("wrow", None, None),
        P("wrow", None, "wcol"),
        P("wcol", "wrow"),
        P("wrow"),
    )
    return jax.shard_map(
        body,
        mesh=mesh,
        in_specs=placed,
        out_specs=P("wrow", ("patch", "wcol"), None),
        check_vma=False,
    )
```

profile of v0, /device:TPU:2, one launch (start us, length us, event | category | flops | bytes accessed | tf_op | source)
XLA Modules:
  0.0 490.6 jit_solution(7066353537932086624)
XLA Ops:
  14.8 29.8 %all-gather.8.cloned.1.call-done = bf16[1,512,1536]{2,1,0:T(8,128)(2,1)} async-done(((bf16[1,128,1536]{2,1,0:T(8,128)(2,1)}), bf16[1,512,1536]{2,1,0:T(8,128)(2,1)}) %all-gather.8.cloned.1.call-update) | async-done | bytes 1572880 | tf_op jit(solution)/shard_map/all_gather | solution.py:54
  44.6 45.2 %all-gather.10.cloned.1.call-done = bf16[1536,3,384]{0,2,1:T(8,128)(2,1)} async-done(((bf16[384,3,384]{0,2,1:T(8,128)(2,1)}), bf16[1536,3,384]{0,2,1:T(8,128)(2,1)}) %all-gather.10.cloned.1.call-update) | async-done | bytes 3538960 | tf_op jit(solution)/shard_map/all_gather | solution.py:58
  89.8 4.7 convolution_convert_fusion
  97.7 103.0 %all-gather.14.cloned.1.call-done = bf16[1,8192,1,384]{1,3,2,0:T(8,128)(2,1)} async-done(((bf16[1,512,1,384]{1,3,2,0:T(8,128)(2,1)}), bf16[1,8192,1,384]{1,3,2,0:T(8,128)(2,1)}) %all-gather.14.cloned.1.call-update) | async-done | bytes 6291472 | tf_op jit(solution)/shard_map/all_gather | solution.py:71
  200.7 104.5 %all-gather.16.cloned.1.call-done = bf16[1,8192,1,384]{1,3,2,0:T(8,128)(2,1)} async-done(((bf16[1,512,1,384]{1,3,2,0:T(8,128)(2,1)}), bf16[1,8192,1,384]{1,3,2,0:T(8,128)(2,1)}) %all-gather.16.cloned.1.call-update) | async-done | bytes 6291472 | tf_op jit(solution)/shard_map/all_gather | solution.py:72
  305.2 143.9 %while.18 = (s32[]{:T(128)}, f32[1,3,512]{2,1,0:T(4,128)S(1)}, f32[1,3,512]{2,1,0:T(4,128)}, f32[1,3,512,128]{3,2,1,0:T(8,128)}, s32[1]{0:T(128)}, /*index=5*/bf...) while((s32[]{:T(128)}, f32[1,3,512]{2,1,0:T(4,128)S(1)}, ...), condition=%wide.region_5.6_spmd.clone, body=%wide.region_2.5_spmd.clone.sunk | while | flops 413477376 | bytes 13930823 | solution.py:82
  309.3 3.2 fusion.46
  318.0 3.5 fusion.46
  327.1 3.4 fusion.46
  336.1 3.4 fusion.46
  345.1 3.4 fusion.46
  354.1 3.4 fusion.46
  363.1 3.4 fusion.46
  372.1 3.4 fusion.46
  381.1 3.4 fusion.46
  390.1 3.4 fusion.46
  399.2 3.4 fusion.46
  408.2 3.4 fusion.46
  417.2 3.4 fusion.46
  426.2 3.4 fusion.46
  435.2 3.4 fusion.46
  444.2 3.4 fusion.46
  451.5 3.4 fusion.17
  454.9 27.0 %reduce-scatter.2.cloned.1.call-done = bf16[1,128,1536]{2,1,0:T(8,128)(2,1)} async-done(((bf16[1,512,1536]{2,1,0:T(8,128)(2,1)}), bf16[1,128,1536]{2,1,0:T(8,128)(2,1)}) %reduce-scatter.2.cloned.1.call-update) | async-done | bytes 393232 | tf_op jit(solution)/shard_map/reduce_scatter | solution.py:93
  (305 shorter events, 103.1 us)
Async XLA Ops:
  6.5 38.1 %all-gather.8.cloned.1.call-start = ((), (), s32[]{:S(2)}) async-start(), calls=%async_computation.1 | async-start | bytes 1966080 | tf_op jit(solution)/shard_map/all_gather | solution.py:54
  12.4 77.4 %all-gather.10.cloned.1.call-start = ((), (), s32[]{:S(2)}) async-start(), calls=%async_computation.2 | async-start | bytes 4423680 | tf_op jit(solution)/shard_map/all_gather | solution.py:58
  14.7 186.0 %all-gather.14.cloned.1.call-start = ((), (), s32[]{:S(2)}) async-start(), calls=%async_computation.5 | async-start | bytes 6684672 | tf_op jit(solution)/shard_map/all_gather | solution.py:71
  96.2 209.0 %all-gather.16.cloned.1.call-start = ((), (), s32[]{:S(2)}) async-start(), calls=%async_computation.6 | async-start | bytes 6684672 | tf_op jit(solution)/shard_map/all_gather | solution.py:72
  96.8 354.7 %all-gather.12.cloned.1.call-start = ((), (), s32[]{:S(2)}) async-start(), calls=%async_computation.3 | async-start | bytes 1474560 | tf_op jit(solution)/shard_map/all_gather | solution.py:89
  97.4 384.6 %reduce-scatter.2.cloned.1.call-start = ((), (), s32[]{:S(2)}) async-start(), calls=%async_computation.4 | async-start | bytes 1966080 | tf_op jit(solution)/shard_map/reduce_scatter | solution.py:93
  318.0 3.5 copy-start.3
  318.0 3.5 copy-start.5
  327.0 3.5 copy-start.3
  336.1 3.5 copy-start.3
  345.1 3.5 copy-start.3
  354.1 3.5 copy-start.3
  363.1 3.5 copy-start.3
  372.1 3.5 copy-start.3
  381.1 3.5 copy-start.3
  390.1 3.5 copy-start.3
  399.1 3.5 copy-start.3
  408.1 3.5 copy-start.3
  417.2 3.5 copy-start.3
  426.2 3.5 copy-start.3
  435.2 3.5 copy-start.3
  444.2 3.5 copy-start.3
  450.6 31.3 %copy-start = (bf16[1,128,1536]{2,1,0:T(8,128)(2,1)S(1)}, bf16[1,128,1536]{2,1,0:T(8,128)(2,1)}, u32[]{:S(2)}) copy-start(bf16[1,128,1536]{2,1,0:T(8,128)(2,1)} %param.7) | copy-start | bytes 1179652
  450.6 31.3 %copy-start.6 = (f32[1536]{0:T(1024)S(1)}, f32[1536]{0:T(1024)}, u32[]{:S(2)}) copy-start(f32[1536]{0:T(1024)} %get-tuple-element.182) | copy-start | bytes 18436
  (64 other events, 91.9 us)
Sparse Core Ops, SparseCore 0:
  12.5 32.0 all-gather.7
  46.4 43.3 all-gather.9
  96.3 104.3 all-gather.13
  203.0 102.2 all-gather.15
  306.9 22.7 all-gather.11
  455.0 26.8 reduce-scatter.1
where the time goes:
time: 492 us; the launch traced here: 491 us
  waiting for transfers between devices  311 us (63%)
  matrix products  76 us (15%)
  local copies, waits for them, and re-layouts  45.7 us (9%)
  other arithmetic  43.1 us (9%)
  between operations  13.6 us (3%)
    all_gather x1, waiting for transfers between devices, body(): value_piece = lax.all_gather(values, 'patch', axis=1, tiled=True)  105 us
    all_gather x1, waiting for transfers between devices, body(): key_piece = lax.all_gather(keys, 'patch', axis=1, tiled=True)  103 us
    dot_general x16, matrix products, absorb(): jnp.einsum('vhqk,vkhd->vhqd', probs.astype(jnp.bfloat16), value_heads, pr...  54.9 us
    all_gather x1, waiting for transfers between devices, body(): piece = lax.all_gather(w_qkv, 'wrow', axis=0, tiled=True)  45.2 us
    dynamic_slice x16, local copies, waits for them, and re-layouts, one_block(): value_block = lax.dynamic_slice_in_dim(value_piece, offset, block_len, 1)  30.6 us
    all_gather x1, waiting for transfers between devices, body(): tile_rows = lax.all_gather(normed, 'wcol', axis=1, tiled=True)  29.8 us
    reduce_scatter x1, waiting for transfers between devices, body(): lax.psum_scatter(partial_out.astype(jnp.bfloat16), 'wcol', scatter_dimens...  27 us
    convert_element_type x16, other arithmetic, absorb(): probs = jnp.exp(scores - new_peak[..., None]) * valid.astype(jnp.float32)  19.9 us
  transfers between devices with their start and end apart: 6, of which 5 were waited for; matrix products, arithmetic and copies ran while one was open for 28% of the time, Pallas kernels for 0%

commit v1 on v0

--- a/solution.py
+++ b/solution.py
@@ -68,7 +68,9 @@
     start_peak = jnp.full((videos_here, heads_here, tile_len), FLOOR, jnp.float32)
     start_sum = jnp.zeros((videos_here, heads_here, tile_len), jnp.float32)
     start_numer = jnp.zeros((videos_here, heads_here, tile_len, HD), jnp.float32)
-    key_piece = lax.all_gather(keys, "patch", axis=1, tiled=True)
+    key_piece = jnp.concatenate(
+        jax.lax.all_to_all(jnp.stack(jax.lax.axis_size("patch") * [keys]), "patch", 0, 0), 1
+    )
     value_piece = lax.all_gather(values, "patch", axis=1, tiled=True)
     count = key_piece.shape[1]
     block_len = 512

time: 492 us -> 528 us (1.073)
  local copies, waits for them, and re-layouts: 45.7 us -> 63.6 us
  matrix products: 76 us -> 90.4 us
  starting transfers between devices: 0.2 us -> 9.26 us
  waiting for transfers between devices: 311 us -> 304 us
    all_to_all x0 -> x1, waiting for transfers between devices: none -> 161 us  [body(): jax.lax.all_to_all(jnp.stack(jax.lax.axis_size('patch') * [keys]), 'patch...]
    all_gather x1 -> x0, waiting for transfers between devices: 103 us -> none  [body(): key_piece = lax.all_gather(keys, 'patch', axis=1, tiled=True)]
    all_gather x1, waiting for transfers between devices: 105 us -> 31.3 us  [body(): value_piece = lax.all_gather(values, 'patch', axis=1, tiled=True)]
    dynamic_slice x0 -> x32, local copies, waits for them, and re-layouts: none -> 19.7 us  [one_block(): key_block = lax.dynamic_slice_in_dim(key_piece, offset, block_len, 1)]
    dot_general x16, matrix products: 13 us -> 29.1 us  [absorb(): jnp.einsum('vqhd,vkhd->vhqk', queries, key_heads, preferred_element_type=...]
    dynamic_slice x16, local copies, waits for them, and re-layouts: 30.6 us -> 16.5 us  [one_block(): value_block = lax.dynamic_slice_in_dim(value_piece, offset, block_len, 1)]
    all_to_all x0 -> x1, starting transfers between devices: none -> 9.1 us  [body(): jax.lax.all_to_all(jnp.stack(jax.lax.axis_size('patch') * [keys]), 'patch...]
    all_to_all x0 -> x1, local copies, waits for them, and re-layouts: none -> 8.67 us  [body(): jax.lax.all_to_all(jnp.stack(jax.lax.axis_size('patch') * [keys]), 'patch...]
  transfers between devices with their start and end apart: 6 -> 6, of which waited for: 5 -> 5; matrix products, arithmetic and copies ran while one was open for 28% -> 32% of each run, Pallas kernels for 0% -> 0%
where the time goes in v1:
time: 528 us; the launch traced here: 525 us
  waiting for transfers between devices  304 us (58%)
  matrix products  90.4 us (17%)
  local copies, waits for them, and re-layouts  63.6 us (12%)
  other arithmetic  42.9 us (8%)
  between operations  13.2 us (2%)
  starting transfers between devices  9.26 us (2%)
    all_to_all x1, waiting for transfers between devices, body(): jax.lax.all_to_all(jnp.stack(jax.lax.axis_size('patch') * [keys]), 'patch...  161 us
    dot_general x16, matrix products, absorb(): jnp.einsum('vhqk,vkhd->vhqd', probs.astype(jnp.bfloat16), value_heads, pr...  53.1 us
    all_gather x1, waiting for transfers between devices, body(): piece = lax.all_gather(w_qkv, 'wrow', axis=0, tiled=True)  45.2 us
    reduce_scatter x1, waiting for transfers between devices, body(): lax.psum_scatter(partial_out.astype(jnp.bfloat16), 'wcol', scatter_dimens...  35.5 us
    all_gather x1, waiting for transfers between devices, body(): value_piece = lax.all_gather(values, 'patch', axis=1, tiled=True)  31.3 us
    all_gather x1, waiting for transfers between devices, body(): tile_rows = lax.all_gather(normed, 'wcol', axis=1, tiled=True)  29.8 us
    dot_general x16, matrix products, absorb(): jnp.einsum('vqhd,vkhd->vhqk', queries, key_heads, preferred_element_type=...  29.1 us
    dynamic_slice x32, local copies, waits for them, and re-layouts, one_block(): key_block = lax.dynamic_slice_in_dim(key_piece, offset, block_len, 1)  19.7 us
  transfers between devices with their start and end apart: 6, of which 5 were waited for; matrix products, arithmetic and copies ran while one was open for 32% of the time, Pallas kernels for 0%

profile of v1, /device:TPU:2, one launch (start us, length us, event | category | flops | bytes accessed | tf_op | source)
XLA Modules:
  0.0 524.5 jit_solution(7805221286097041953)
XLA Ops:
  14.8 29.8 %all-gather.6.cloned.1.call-done = bf16[1,512,1536]{2,1,0:T(8,128)(2,1)} async-done(((bf16[1,128,1536]{2,1,0:T(8,128)(2,1)}), bf16[1,512,1536]{2,1,0:T(8,128)(2,1)}) %all-gather.6.cloned.1.call-update) | async-done | bytes 1572880 | tf_op jit(solution)/shard_map/all_gather | solution.py:54
  44.6 45.2 %all-gather.8.cloned.1.call-done = bf16[1536,3,384]{0,2,1:T(8,128)(2,1)} async-done(((bf16[384,3,384]{0,2,1:T(8,128)(2,1)}), bf16[1536,3,384]{0,2,1:T(8,128)(2,1)}) %all-gather.8.cloned.1.call-update) | async-done | bytes 3538960 | tf_op jit(solution)/shard_map/all_gather | solution.py:58
  89.8 4.7 convolution_convert_fusion
  99.3 9.1 %all-to-all-start = ((bf16[16,1,512,384]{2,3,1,0:T(8,128)(2,1)}), bf16[16,1,512,384]{2,3,1,0:T(8,128)(2,1)}, u32[]{:S(2)}, u32[]{:S(2)}) async-start(bf16[16,1,512,384]{2,3,1,0:T(8,128)(2,1)} %stack.3), calls=%async_computation | async-start | bytes 12582912 | tf_op jit(solution)/shard_map/all_to_all | solution.py:72
  109.9 161.3 %all-to-all-done = bf16[16,1,512,384]{2,3,1,0:T(8,128)(2,1)} async-done(((bf16[16,1,512,384]{2,3,1,0:T(8,128)(2,1)}), bf16[16,1,512,384]{2,3,1,0:T(8,128)(2,1)}, u32[]{:S(2)}, u32[]{:S(2)}) %all-to-all-start) | async-done | bytes 6291488 | tf_op jit(solution)/shard_map/all_to_all | solution.py:72
  271.2 8.7 %copy.33 = bf16[16,1,512,384]{3,2,0,1:T(8,128)(2,1)} copy(bf16[16,1,512,384]{2,3,1,0:T(8,128)(2,1)} %all-to-all-done) | data formatting | bytes 12582912 | tf_op jit(solution)/shard_map/all_to_all | solution.py:72
  279.9 31.3 %all-gather.12.cloned.1.call-done = bf16[1,8192,1,384]{1,3,2,0:T(8,128)(2,1)} async-done(((bf16[1,512,1,384]{1,3,2,0:T(8,128)(2,1)}), bf16[1,8192,1,384]{1,3,2,0:T(8,128)(2,1)}) %all-gather.12.cloned.1.call-update) | async-done | bytes 6291472 | tf_op jit(solution)/shard_map/all_gather | solution.py:74
  311.2 163.7 %while.18 = (s32[]{:T(128)}, f32[1,3,512]{2,1,0:T(4,128)S(1)}, f32[1,3,512]{2,1,0:T(4,128)}, f32[1,3,512,128]{3,2,1,0:T(8,128)}, s32[1]{0:T(128)}, /*index=5*/bf...) while((s32[]{:T(128)}, f32[1,3,512]{2,1,0:T(4,128)S(1)}, ...), condition=%wide.region_5.6_spmd.clone, body=%wide.region_2.5_spmd.clone.sunk | while | flops 413477376 | bytes 14717259 | solution.py:84
  326.4 3.3 fusion.46
  336.7 3.4 fusion.46
  347.0 3.3 fusion.46
  357.2 3.3 fusion.46
  367.5 3.3 fusion.46
  377.7 3.3 fusion.46
  388.0 3.3 fusion.46
  398.2 3.3 fusion.46
  408.5 3.3 fusion.46
  418.8 3.3 fusion.46
  429.0 3.3 fusion.46
  439.3 3.3 fusion.46
  449.5 3.3 fusion.46
  470.0 3.3 fusion.46
  477.2 3.4 fusion.17
  480.7 35.5 %reduce-scatter.2.cloned.1.call-done = bf16[1,128,1536]{2,1,0:T(8,128)(2,1)} async-done(((bf16[1,512,1536]{2,1,0:T(8,128)(2,1)}), bf16[1,128,1536]{2,1,0:T(8,128)(2,1)}) %reduce-scatter.2.cloned.1.call-update) | async-done | bytes 393232 | tf_op jit(solution)/shard_map/reduce_scatter | solution.py:95
  (338 shorter events, 133.9 us)
Async XLA Ops:
  6.5 38.1 %all-gather.6.cloned.1.call-start = ((), (), s32[]{:S(2)}) async-start(), calls=%async_computation.2 | async-start | bytes 1966080 | tf_op jit(solution)/shard_map/all_gather | solution.py:54
  12.4 77.4 %all-gather.8.cloned.1.call-start = ((), (), s32[]{:S(2)}) async-start(), calls=%async_computation.3 | async-start | bytes 4423680 | tf_op jit(solution)/shard_map/all_gather | solution.py:58
  14.7 296.4 %all-gather.12.cloned.1.call-start = ((), (), s32[]{:S(2)}) async-start(), calls=%async_computation.6 | async-start | bytes 6684672 | tf_op jit(solution)/shard_map/all_gather | solution.py:74
  99.3 171.9 %all-to-all-start = ((bf16[16,1,512,384]{2,3,1,0:T(8,128)(2,1)}), bf16[16,1,512,384]{2,3,1,0:T(8,128)(2,1)}, u32[]{:S(2)}, u32[]{:S(2)}) async-start(bf16[16,1,512,384]{2,3,1,0:T(8,128)(2,1)} %stack.3), calls=%async_computation | async-start | bytes 12582912 | tf_op jit(solution)/shard_map/all_to_all | solution.py:72
  108.4 368.8 %all-gather.10.cloned.1.call-start = ((), (), s32[]{:S(2)}) async-start(), calls=%async_computation.4 | async-start | bytes 1474560 | tf_op jit(solution)/shard_map/all_gather | solution.py:91
  108.9 407.2 %reduce-scatter.2.cloned.1.call-start = ((), (), s32[]{:S(2)}) async-start(), calls=%async_computation.5 | async-start | bytes 1966080 | tf_op jit(solution)/shard_map/reduce_scatter | solution.py:95
  326.4 3.4 copy-start.3
  336.7 3.4 copy-start.3
  336.7 3.4 copy-start.5
  346.9 3.4 copy-start.3
  357.2 3.4 copy-start.3
  367.4 3.4 copy-start.3
  377.7 3.4 copy-start.3
  388.0 3.4 copy-start.3
  398.2 3.4 copy-start.3
  408.5 3.4 copy-start.3
  418.7 3.4 copy-start.3
  429.0 3.4 copy-start.3
  439.2 3.4 copy-start.3
  449.5 3.4 copy-start.3
  459.8 3.4 copy-start.3
  470.0 3.4 copy-start.3
  476.3 39.8 %copy-start = (bf16[1,128,1536]{2,1,0:T(8,128)(2,1)S(1)}, bf16[1,128,1536]{2,1,0:T(8,128)(2,1)}, u32[]{:S(2)}) copy-start(bf16[1,128,1536]{2,1,0:T(8,128)(2,1)} %param.7) | copy-start | bytes 1179652
  476.3 39.8 %copy-start.6 = (f32[1536]{0:T(1024)S(1)}, f32[1536]{0:T(1024)}, u32[]{:S(2)}) copy-start(f32[1536]{0:T(1024)} %get-tuple-element.198) | copy-start | bytes 18436
  (64 other events, 106.0 us)
Sparse Core Ops, SparseCore 0:
  12.5 32.0 all-gather.5
  46.4 43.3 all-gather.7
  96.1 214.9 all-gather.11
  312.9 31.2 all-gather.9
  480.8 35.3 reduce-scatter.1
